TPU v7x, 128 devices: a whole 4x4x4 slice. The times are simulated.
128 devices in a mesh: row: 64 (over y_hi, z, x, core), rep: 2 (over y_lo).
Axes of the slice: x: 4, y: 4 (y_hi: 2, y_lo: 2; y = y_hi * 2 + y_lo), z: 4, core: 2. Of those that a mesh axis runs over, the one named last changes fastest.
Arguments:
- features: bfloat16 [131072, 256], P('row'), may hold values from -6 to 6
- adjacency: bfloat16 [1024, 48, 128, 128], P('row', 'rep'), may hold values from 0 to 3, as said below
- columns: int32 [1024, 48], P('row', 'rep'), may hold values from 0 to 1023, as said below
- live: int32 [1024], P('row'), may hold values from 0 to 48, as said below
- w_self: bfloat16 [256, 256], replicated, may hold values from -0.375 to 0.375
- w_neigh: bfloat16 [256, 256], replicated, may hold values from -4 to 4
- bias: float32 [256], replicated, may hold values from -3 to 3
Outputs:
- mixed: bfloat16 [131072, 256], P(('row', 'rep'))
Inputs may be any that keep to these rules, and one draw needn't show every extreme that they name: `adjacency`: edge weights are nonnegative; most entries are zero, and some nodes have no edges at all. `columns`: the column block of every slot of block row b lies in the block rows held by a row index at most 2 away from the one holding b (never outside the graph). Slots at or after live[b] are ignored; some block row uses all 48 slots.
All inputs are finite; a program needn't handle non-finite values.
Results may differ from a plain program's by a relative error of at most 0.0048.
Values may be sent and summed in bfloat16 or wider, within the bound.
A program may use at most 64 MiB of HBM per device.

v0:
```python
import jax
import jax.numpy as jnp
from jax import lax
from jax.sharding import PartitionSpec as P

REACH = 2


def shifted(block, axis, distance):
    devices = range(lax.axis_size(axis))
    route = [(i - distance, i) for i in devices if i - distance in devices]
    return lax.ppermute(block, axis, route)


def tile_products(tiles, window_index, counts, first_slot, window):
    slot_total = tiles.shape[1]
    feature_width = window.shape[2]
    usable = jnp.clip(counts - first_slot, 0, slot_total)

    def one_row(row_item):
        row_tiles, row_index, row_count = row_item
        live_slots = jnp.arange(slot_total, dtype=jnp.int32) < row_count
        masked = jnp.where(live_slots[:, None, None], row_tiles, jnp.zeros((), row_tiles.dtype))
        source = window[row_index]
        running = jnp.einsum("sij,sjf->if", masked, source, preferred_element_type=jnp.float32)
        degree = jnp.sum(masked, axis=(0, 2), dtype=jnp.float32)
        return (running, degree)

    totals, degrees = lax.map(one_row, (tiles, window_index, usable))
    return (totals.reshape(-1, feature_width), degrees.reshape(-1))


def local(features, adjacency, columns, live, w_self, w_neigh, bias):
    feature_width = features.shape[1]
    tile_edge = adjacency.shape[2]
    own_blocks = features.shape[0] // tile_edge
    own_feats = features.reshape(own_blocks, tile_edge, feature_width)
    row_place = lax.axis_index("row")
    replica = lax.axis_index("rep")
    sharers = lax.axis_size("rep")
    nearby = {0: own_feats}
    for offset in range(-REACH, REACH + 1):
        if offset != 0:
            nearby[offset] = shifted(own_feats, "row", -offset)
    window = jnp.concatenate([nearby[offset] for offset in range(-REACH, REACH + 1)], axis=0)
    window_index = (columns // own_blocks - row_place + REACH) * own_blocks + columns % own_blocks
    out_rows = own_blocks * tile_edge // sharers
    totals, degrees = tile_products(
        adjacency, window_index, live, replica * columns.shape[1], window
    )
    totals, degrees = (
        lax.psum_scatter(totals, "rep", scatter_dimension=0, tiled=True),
        lax.psum_scatter(degrees, "rep", scatter_dimension=0, tiled=True),
    )
    own_rows = lax.dynamic_slice_in_dim(features, replica * out_rows, out_rows, 0)
    neighbor_mean = (totals / jnp.maximum(degrees, 1.0)[:, None]).astype(jnp.bfloat16)
    summed = jnp.dot(own_rows, w_self, preferred_element_type=jnp.float32)
    summed = summed + jnp.dot(neighbor_mean, w_neigh, preferred_element_type=jnp.float32) + bias
    return jax.nn.relu(summed).astype(jnp.bfloat16)


def solution(mesh):
    placed = (P("row", None), P("row", "rep", None, None), P("row", "rep"), P("row"), P(), P(), P())
    return jax.shard_map(
        local, mesh=mesh, in_specs=placed, out_specs=P(("row", "rep"), None), check_vma=False
    )
```

profile of v0, /device:TPU:102, one launch (start us, length us, event | category | flops | bytes accessed | tf_op | source)
XLA Modules:
  0.0 233.2 jit_solution(12525107700230701791)
XLA Ops:
  6.5 3.8 %collective-permute-start = (bf16[16,128,256]{2,1,0:T(8,128)(2,1)}, bf16[16,128,256]{2,1,0:T(8,128)(2,1)}, u32[]{:S(2)}, u32[]{:S(2)}) collective-permute-start(bf16[16,128,256]{2,1,0:T(8,128)(2,1)} %bitcast.43), channel_id=1, source_target_pairs={{0,4},{2,6},{4,8},{6,10},{8,12},{10,14},{12,16},{14,18},{16,20},{1... | collective-permute-start | bytes 3145736 | tf_op jit(solution)/shard_map/ppermute | solution.py:12
  12.3 3.6 %collective-permute-start.2 = (bf16[16,128,256]{2,1,0:T(8,128)(2,1)}, bf16[16,128,256]{2,1,0:T(8,128)(2,1)S(1)}, u32[]{:S(2)}, u32[]{:S(2)}) collective-permute-start(bf16[16,128,256]{2,1,0:T(8,128)(2,1)} %bitcast.45), channel_id=1, source_target_pairs={{2,0},{4,2},{6,4},{8,6},{10,8},{12,10},{14,12},{16,14},{18,16},{20... | collective-permute-start | bytes 3145736 | tf_op jit(solution)/shard_map/ppermute | solution.py:12
  19.5 15.4 %collective-permute-done = bf16[16,128,256]{2,1,0:T(8,128)(2,1)} collective-permute-done((bf16[16,128,256]{2,1,0:T(8,128)(2,1)}, bf16[16,128,256]{2,1,0:T(8,128)(2,1)}, u32[]{:S(2)}, u32[]{:S(2)}) %collective-permute-start) | collective-permute-done | bytes 1048608 | tf_op jit(solution)/shard_map/ppermute | solution.py:12
  36.2 8.7 %collective-permute-done.1 = bf16[16,128,256]{2,1,0:T(8,128)(2,1)S(1)} collective-permute-done((bf16[16,128,256]{2,1,0:T(8,128)(2,1)}, bf16[16,128,256]{2,1,0:T(8,128)(2,1)S(1)}, u32[]{:S(2)}, u32[]{:S(2)}) %collective-permute-start.1) | collective-permute-done | bytes 1048608 | tf_op jit(solution)/shard_map/ppermute | solution.py:12
  46.4 12.2 %collective-permute-done.3 = bf16[16,128,256]{2,1,0:T(8,128)(2,1)S(1)} collective-permute-done((bf16[16,128,256]{2,1,0:T(8,128)(2,1)}, bf16[16,128,256]{2,1,0:T(8,128)(2,1)S(1)}, u32[]{:S(2)}, u32[]{:S(2)}) %collective-permute-start.3) | collective-permute-done | bytes 1048608 | tf_op jit(solution)/shard_map/ppermute | solution.py:12
  58.6 2.3 copy-done.1
  60.9 130.0 %while.12 = (s32[]{:T(128)}, f32[16,128,256]{2,1,0:T(8,128)}, f32[16,128]{1,0:T(8,128)S(1)}, s32[16]{0:T(128)S(1)}, bf16[16,24,128,128]{3,2,1,0:T(8,128)(2,1)}, ...) while((s32[]{:T(128)}, f32[16,128,256]{2,1,0:T(8,128)}, ...), condition=%wide.region_2.3_spmd, body=%wide.region_0.2_spmd.sunk | while | flops 202900448 | bytes 6429761 | solution.py:29
  61.0 3.2 %gather_fusion = bf16[24,128,256]{2,1,0:T(8,128)(2,1)S(1)} fusion(bf16[80,128,256]{2,1,0:T(8,128)(2,1)} %get-tuple-element.126, s32[1024]{0:T(1024)S(1)} %pad_clamp_fusion.2), kind=kCustom, calls=%fused_computation.clone.1 | custom fusion | bytes 3145824 | tf_op jit(solution)/shard_map/while/body/eval_jaxpr/gather | solution.py:24
  69.2 3.1 %gather_fusion = bf16[24,128,256]{2,1,0:T(8,128)(2,1)S(1)} fusion(bf16[80,128,256]{2,1,0:T(8,128)(2,1)} %get-tuple-element.126, s32[1024]{0:T(1024)S(1)} %pad_clamp_fusion.2), kind=kCustom, calls=%fused_computation.clone.1 | custom fusion | bytes 3145824 | tf_op jit(solution)/shard_map/while/body/eval_jaxpr/gather | solution.py:24
  73.6 2.2 fusion.28
  77.3 3.1 %gather_fusion = bf16[24,128,256]{2,1,0:T(8,128)(2,1)S(1)} fusion(bf16[80,128,256]{2,1,0:T(8,128)(2,1)} %get-tuple-element.126, s32[1024]{0:T(1024)S(1)} %pad_clamp_fusion.2), kind=kCustom, calls=%fused_computation.clone.1 | custom fusion | bytes 3145824 | tf_op jit(solution)/shard_map/while/body/eval_jaxpr/gather | solution.py:24
  85.4 3.1 %gather_fusion = bf16[24,128,256]{2,1,0:T(8,128)(2,1)S(1)} fusion(bf16[80,128,256]{2,1,0:T(8,128)(2,1)} %get-tuple-element.126, s32[1024]{0:T(1024)S(1)} %pad_clamp_fusion.2), kind=kCustom, calls=%fused_computation.clone.1 | custom fusion | bytes 3145824 | tf_op jit(solution)/shard_map/while/body/eval_jaxpr/gather | solution.py:24
  93.6 3.1 %gather_fusion = bf16[24,128,256]{2,1,0:T(8,128)(2,1)S(1)} fusion(bf16[80,128,256]{2,1,0:T(8,128)(2,1)} %get-tuple-element.126, s32[1024]{0:T(1024)S(1)} %pad_clamp_fusion.2), kind=kCustom, calls=%fused_computation.clone.1 | custom fusion | bytes 3145824 | tf_op jit(solution)/shard_map/while/body/eval_jaxpr/gather | solution.py:24
  97.9 2.2 fusion.28
  101.7 3.1 %gather_fusion = bf16[24,128,256]{2,1,0:T(8,128)(2,1)S(1)} fusion(bf16[80,128,256]{2,1,0:T(8,128)(2,1)} %get-tuple-element.126, s32[1024]{0:T(1024)S(1)} %pad_clamp_fusion.2), kind=kCustom, calls=%fused_computation.clone.1 | custom fusion | bytes 3145824 | tf_op jit(solution)/shard_map/while/body/eval_jaxpr/gather | solution.py:24
  109.8 3.1 %gather_fusion = bf16[24,128,256]{2,1,0:T(8,128)(2,1)S(1)} fusion(bf16[80,128,256]{2,1,0:T(8,128)(2,1)} %get-tuple-element.126, s32[1024]{0:T(1024)S(1)} %pad_clamp_fusion.2), kind=kCustom, calls=%fused_computation.clone.1 | custom fusion | bytes 3145824 | tf_op jit(solution)/shard_map/while/body/eval_jaxpr/gather | solution.py:24
  114.2 2.2 fusion.28
  117.9 3.1 %gather_fusion = bf16[24,128,256]{2,1,0:T(8,128)(2,1)S(1)} fusion(bf16[80,128,256]{2,1,0:T(8,128)(2,1)} %get-tuple-element.126, s32[1024]{0:T(1024)S(1)} %pad_clamp_fusion.2), kind=kCustom, calls=%fused_computation.clone.1 | custom fusion | bytes 3145824 | tf_op jit(solution)/shard_map/while/body/eval_jaxpr/gather | solution.py:24
  126.0 3.1 %gather_fusion = bf16[24,128,256]{2,1,0:T(8,128)(2,1)S(1)} fusion(bf16[80,128,256]{2,1,0:T(8,128)(2,1)} %get-tuple-element.126, s32[1024]{0:T(1024)S(1)} %pad_clamp_fusion.2), kind=kCustom, calls=%fused_computation.clone.1 | custom fusion | bytes 3145824 | tf_op jit(solution)/shard_map/while/body/eval_jaxpr/gather | solution.py:24
  134.2 3.1 %gather_fusion = bf16[24,128,256]{2,1,0:T(8,128)(2,1)S(1)} fusion(bf16[80,128,256]{2,1,0:T(8,128)(2,1)} %get-tuple-element.126, s32[1024]{0:T(1024)S(1)} %pad_clamp_fusion.2), kind=kCustom, calls=%fused_computation.clone.1 | custom fusion | bytes 3145824 | tf_op jit(solution)/shard_map/while/body/eval_jaxpr/gather | solution.py:24
  142.3 3.1 %gather_fusion = bf16[24,128,256]{2,1,0:T(8,128)(2,1)S(1)} fusion(bf16[80,128,256]{2,1,0:T(8,128)(2,1)} %get-tuple-element.126, s32[1024]{0:T(1024)S(1)} %pad_clamp_fusion.2), kind=kCustom, calls=%fused_computation.clone.1 | custom fusion | bytes 3145824 | tf_op jit(solution)/shard_map/while/body/eval_jaxpr/gather | solution.py:24
  150.4 3.1 %gather_fusion = bf16[24,128,256]{2,1,0:T(8,128)(2,1)S(1)} fusion(bf16[80,128,256]{2,1,0:T(8,128)(2,1)} %get-tuple-element.126, s32[1024]{0:T(1024)S(1)} %pad_clamp_fusion.2), kind=kCustom, calls=%fused_computation.clone.1 | custom fusion | bytes 3145824 | tf_op jit(solution)/shard_map/while/body/eval_jaxpr/gather | solution.py:24
  154.8 2.2 fusion.28
  158.5 3.1 %gather_fusion = bf16[24,128,256]{2,1,0:T(8,128)(2,1)S(1)} fusion(bf16[80,128,256]{2,1,0:T(8,128)(2,1)} %get-tuple-element.126, s32[1024]{0:T(1024)S(1)} %pad_clamp_fusion.2), kind=kCustom, calls=%fused_computation.clone.1 | custom fusion | bytes 3145824 | tf_op jit(solution)/shard_map/while/body/eval_jaxpr/gather | solution.py:24
  162.9 2.2 fusion.28
  166.7 3.1 %gather_fusion = bf16[24,128,256]{2,1,0:T(8,128)(2,1)S(1)} fusion(bf16[80,128,256]{2,1,0:T(8,128)(2,1)} %get-tuple-element.126, s32[1024]{0:T(1024)S(1)} %pad_clamp_fusion.2), kind=kCustom, calls=%fused_computation.clone.1 | custom fusion | bytes 3145824 | tf_op jit(solution)/shard_map/while/body/eval_jaxpr/gather | solution.py:24
  174.8 3.1 %gather_fusion = bf16[24,128,256]{2,1,0:T(8,128)(2,1)S(1)} fusion(bf16[80,128,256]{2,1,0:T(8,128)(2,1)} %get-tuple-element.126, s32[1024]{0:T(1024)S(1)} %pad_clamp_fusion.2), kind=kCustom, calls=%fused_computation.clone.1 | custom fusion | bytes 3145824 | tf_op jit(solution)/shard_map/while/body/eval_jaxpr/gather | solution.py:24
  179.2 2.2 fusion.28
  182.9 3.1 %gather_fusion = bf16[24,128,256]{2,1,0:T(8,128)(2,1)S(1)} fusion(bf16[80,128,256]{2,1,0:T(8,128)(2,1)} %get-tuple-element.126, s32[1024]{0:T(1024)S(1)} %pad_clamp_fusion.2), kind=kCustom, calls=%fused_computation.clone.1 | custom fusion | bytes 3145824 | tf_op jit(solution)/shard_map/while/body/eval_jaxpr/gather | solution.py:24
  192.6 5.0 %all-reduce = f32[2048]{0:T(1024)S(1)} all-reduce(f32[2048]{0:T(1024)S(1)} %bitcast.50), channel_id=3, replica_groups=mesh['row'=64,'rep'=2] {'rep'}, use_global_device_ids=true, to_apply=%region_4.5.clone | all-reduce | flops 2048 | bytes 16384
  197.6 26.4 %reduce-scatter.2.cloned.1.call-done = f32[1024,256]{1,0:T(8,128)} async-done(((f32[2048,256]{1,0:T(8,128)}), f32[1024,256]{1,0:T(8,128)}) %reduce-scatter.2.cloned.1.call-update) | async-done | bytes 1048592 | tf_op jit(solution)/shard_map/reduce_scatter | solution.py:52
  224.0 2.4 %fusion.7 = bf16[1024,256]{1,0:T(8,128)(2,1)} fusion(f32[1024,256]{1,0:T(8,128)S(1)} %fusion.9, bf16[256,256]{1,0:T(8,128)(2,1)S(1)} %copy-done.3, f32[1024,256]{1,0:T(8,128)} %reduce-scatter.2.cloned.1.call-done, f32[256]{0:T(256)S(1)} %copy-done.4, f32[1024]{0:T(1024)S(1)} %dynamic-slice_maximum_fusion), kind=kOutput, calls=%fused_computation.16 | convolution fusion | flops 135790592 | bytes 2757632 | tf_op jit(solution)/shard_map/dot_general | solution.py:58
  (134 shorter events, 75.0 us)
Async XLA Ops:
  6.5 185.7 %copy-start = (bf16[256,256]{1,0:T(8,128)(2,1)S(1)}, bf16[256,256]{1,0:T(8,128)(2,1)}, u32[]{:S(2)}) copy-start(bf16[256,256]{1,0:T(8,128)(2,1)} %param.13) | copy-start | bytes 393220
  6.5 217.4 %reduce-scatter.2.cloned.1.call-start = ((), (), s32[]{:S(2)}) async-start(), calls=%async_computation.1 | async-start | bytes 3145728 | tf_op jit(solution)/shard_map/reduce_scatter | solution.py:52
  6.5 28.4 %collective-permute-start = (bf16[16,128,256]{2,1,0:T(8,128)(2,1)}, bf16[16,128,256]{2,1,0:T(8,128)(2,1)}, u32[]{:S(2)}, u32[]{:S(2)}) collective-permute-start(bf16[16,128,256]{2,1,0:T(8,128)(2,1)} %bitcast.43), channel_id=1, source_target_pairs={{0,4},{2,6},{4,8},{6,10},{8,12},{10,14},{12,16},{14,18},{16,20},{1... | collective-permute-start | bytes 3145736 | tf_op jit(solution)/shard_map/ppermute | solution.py:12
  10.3 34.6 %collective-permute-start.1 = (bf16[16,128,256]{2,1,0:T(8,128)(2,1)}, bf16[16,128,256]{2,1,0:T(8,128)(2,1)S(1)}, u32[]{:S(2)}, u32[]{:S(2)}) collective-permute-start(bf16[16,128,256]{2,1,0:T(8,128)(2,1)} %bitcast.44), channel_id=1, source_target_pairs={{0,2},{2,4},{4,6},{6,8},{8,10},{10,12},{12,14},{14,16},{16,18},{18... | collective-permute-start | bytes 3145736 | tf_op jit(solution)/shard_map/ppermute | solution.py:12
  12.3 34.0 %collective-permute-start.2 = (bf16[16,128,256]{2,1,0:T(8,128)(2,1)}, bf16[16,128,256]{2,1,0:T(8,128)(2,1)S(1)}, u32[]{:S(2)}, u32[]{:S(2)}) collective-permute-start(bf16[16,128,256]{2,1,0:T(8,128)(2,1)} %bitcast.45), channel_id=1, source_target_pairs={{2,0},{4,2},{6,4},{8,6},{10,8},{12,10},{14,12},{16,14},{18,16},{20... | collective-permute-start | bytes 3145736 | tf_op jit(solution)/shard_map/ppermute | solution.py:12
  15.9 42.6 %collective-permute-start.3 = (bf16[16,128,256]{2,1,0:T(8,128)(2,1)}, bf16[16,128,256]{2,1,0:T(8,128)(2,1)S(1)}, u32[]{:S(2)}, u32[]{:S(2)}) collective-permute-start(bf16[16,128,256]{2,1,0:T(8,128)(2,1)} %bitcast.46), channel_id=1, source_target_pairs={{4,0},{6,2},{8,4},{10,6},{12,8},{14,10},{16,12},{18,14},{20,16},{2... | collective-permute-start | bytes 3145736 | tf_op jit(solution)/shard_map/ppermute | solution.py:12
  58.6 2.3 copy-start.1
  60.9 130.1 %copy-start.5 = (u32[128]{0:T(128)S(1)}, u32[128]{0:T(128)}, u32[]{:S(2)}) copy-start(u32[128]{0:T(128)} %constant.78) | copy-start | bytes 1540
  60.9 131.4 %copy-start.2 = (bf16[2048,256]{1,0:T(8,128)(2,1)S(1)}, bf16[2048,256]{1,0:T(8,128)(2,1)}, u32[]{:S(2)}) copy-start(bf16[2048,256]{1,0:T(8,128)(2,1)} %param.9) | copy-start | bytes 3145732
  60.9 163.0 %copy-start.3 = (bf16[256,256]{1,0:T(8,128)(2,1)S(1)}, bf16[256,256]{1,0:T(8,128)(2,1)}, u32[]{:S(2)}) copy-start(bf16[256,256]{1,0:T(8,128)(2,1)} %param.14) | copy-start | bytes 393220
  60.9 163.0 %copy-start.4 = (f32[256]{0:T(256)S(1)}, f32[256]{0:T(256)}, u32[]{:S(2)}) copy-start(f32[256]{0:T(256)} %param.15) | copy-start | bytes 3076
Sparse Core Ops, SparseCore 0:
  191.1 32.7 reduce-scatter.1
where the time goes:
time: 238 us; the launch traced here: 233 us
  local copies, waits for them, and re-layouts  66 us (28%)
  waiting for transfers between devices  62.7 us (26%)
  matrix products  38.1 us (16%)
  other arithmetic  35 us (15%)
  between operations  14.2 us (6%)
  starting transfers between devices  11.5 us (5%)
  blocking collectives  5.01 us (2%)
    gather x16, local copies, waits for them, and re-layouts, one_row(): source = window[row_index]  50.2 us
    ppermute x4, waiting for transfers between devices, shifted(): return lax.ppermute(block, axis, route)  36.3 us
    dot_general x16, matrix products, one_row(): jnp.einsum('sij,sjf->if', masked, source, preferred_element_type=jnp.floa...  35.4 us
    reduce_scatter x1, waiting for transfers between devices, local(): lax.psum_scatter(totals, 'rep', scatter_dimension=0, tiled=True)  26.4 us
    reduce_sum x16, other arithmetic, one_row(): degree = jnp.sum(masked, axis=(0, 2), dtype=jnp.float32)  23.3 us
    ppermute x4, starting transfers between devices, shifted(): return lax.ppermute(block, axis, route)  11.5 us
    lt x16, other arithmetic, one_row(): live_slots = jnp.arange(slot_total, dtype=jnp.int32) < row_count  10 us
    dynamic_slice x16, local copies, waits for them, and re-layouts, tile_products(): totals, degrees = lax.map(one_row, (tiles, window_index, usable))  9.59 us
  transfers between devices with their start and end apart: 5, of which 4 were waited for; matrix products, arithmetic and copies ran while one was open for 2% of the time, Pallas kernels for 0%

commit v1 on v0

v1 whole, which is shorter than its diff:
```python
import functools

import jax
import jax.numpy as jnp
from jax import lax
from jax.experimental import pallas as pl
from jax.experimental.pallas import tpu as pltpu
from jax.sharding import PartitionSpec as P

REACH = 2
LANES = 128
PIECES = 4
MESH = pl.DeviceIdType.MESH


def kernel(
    row_total, feats, adjacency, columns, live, w_self, w_neigh, bias, out,
    win_low, win_high, tiles, partial_out, partial_in, own_totals, base, inverse, degree_out, degree_in,
    tile_sem, own_sem, send_sem, recv_sem, part_send, part_recv, degree_sems,
):
    block_rows, slots, edge, _ = tiles.shape
    width = feats.shape[2]
    chunks = width // LANES
    piece = block_rows // PIECES
    half = block_rows // 2
    zero_block = (2 * REACH + 1) * block_rows
    win = (win_low, win_high)

    me = lax.axis_index("row")
    rep = lax.axis_index("rep")
    core = lax.rem(me, 2)
    mate = me + 1 - 2 * core
    other = 1 - rep
    has_next = me + 2 < row_total
    has_prev = me >= 2
    chip = me // 2
    middle = row_total // 4
    rep_next = jnp.where(chip == middle - 1, other, rep)
    rep_prev = jnp.where(chip == middle, other, rep)
    relay_out = jnp.where(core == 0, me + 2 < row_total, me >= 2)
    relay_in = jnp.where(core == 0, me >= 2, me + 2 < row_total)

    def tile_copy(b):
        return pltpu.make_async_copy(adjacency.at[b], tiles.at[b], tile_sem.at[b])

    def own_copy(c):
        return pltpu.make_async_copy(
            feats.at[:, :, pl.ds(c * LANES, LANES)],
            win[c].at[pl.ds(REACH * block_rows, block_rows)],
            own_sem.at[c],
        )

    def remote(flow, c, k, src, slot, device):
        return pltpu.make_async_remote_copy(
            src_ref=src,
            dst_ref=win[c].at[pl.ds(slot * block_rows + k * piece, piece)],
            send_sem=send_sem.at[flow, c, k],
            recv_sem=recv_sem.at[flow, c, k],
            device_id=device,
            device_id_type=MESH,
        )

    def own_piece(c, k):
        return feats.at[pl.ds(k * piece, piece), :, pl.ds(c * LANES, LANES)]

    def to_next(c, k):
        return remote(0, c, k, own_piece(c, k), 0, (me + 2, rep_next))

    def to_prev(c, k):
        return remote(1, c, k, own_piece(c, k), 4, (me - 2, rep_prev))

    def to_mate(c, k):
        return remote(2, c, k, own_piece(c, k), 1 + 2 * core, (mate, rep))

    def relay(c, k):
        start = (4 - 4 * core) * block_rows + k * piece
        return remote(3, c, k, win[c].at[pl.ds(start, piece)], 3 - 2 * core, (mate, rep))

    def arrived(flow, c, k):
        remote(flow, c, k, own_piece(c, k), 0, (mate, rep)).wait_recv()

    def part_copy(c, i):
        return pltpu.make_async_remote_copy(
            src_ref=partial_out.at[c, i],
            dst_ref=partial_in.at[c, i],
            send_sem=part_send.at[c, i],
            recv_sem=part_recv.at[c, i],
            device_id=(me, other),
            device_id_type=MESH,
        )

    degree_copy = pltpu.make_async_remote_copy(
        src_ref=degree_out,
        dst_ref=degree_in,
        send_sem=degree_sems.at[0],
        recv_sem=degree_sems.at[1],
        device_id=(me, other),
        device_id_type=MESH,
    )

    for c in range(chunks):
        own_copy(c).start()
    for b in range(block_rows):
        tile_copy(b).start()

    barrier = pltpu.get_barrier_semaphore()
    pl.semaphore_signal(barrier, inc=1, device_id=(mate, rep), device_id_type=MESH)
    pl.semaphore_signal(barrier, inc=1, device_id=(me, other), device_id_type=MESH)

    @pl.when(has_next)
    def _():
        pl.semaphore_signal(barrier, inc=1, device_id=(me + 2, rep_next), device_id_type=MESH)

    @pl.when(has_prev)
    def _():
        pl.semaphore_signal(barrier, inc=1, device_id=(me - 2, rep_prev), device_id_type=MESH)

    pl.semaphore_wait(barrier, 2 + has_next.astype(jnp.int32) + has_prev.astype(jnp.int32))

    for c in range(chunks):
        for k in range(PIECES):

            @pl.when(has_next)
            def _():
                to_next(c, k).start()

            @pl.when(has_prev)
            def _():
                to_prev(c, k).start()

            to_mate(c, k).start()

    lane = lax.broadcasted_iota(jnp.int32, (edge, LANES), 1)
    first_slot = rep * slots
    for c in range(chunks):
        win[c][zero_block] = jnp.zeros((edge, LANES), win[c].dtype)

    def within(s, used):
        return jnp.minimum(jnp.maximum(used - s, 0), 1)

    def degree_of(b, i, held):
        tile_copy(b).wait()
        used = live[0, b] - first_slot
        total = jnp.zeros((edge, edge), jnp.float32)
        for s in range(slots):
            total += tiles[b, s].astype(jnp.float32) * within(s, used).astype(jnp.float32)
        return jnp.where(lane == i, jnp.sum(total, axis=1, keepdims=True), held)

    no_degrees = jnp.zeros((edge, LANES), jnp.float32)
    degree_out[...] = lax.fori_loop(
        0, half, lambda i, held: degree_of(other * half + i, i, held), no_degrees
    )
    own_degrees = lax.fori_loop(
        0, half, lambda i, held: degree_of(rep * half + i, i, held), no_degrees
    )
    degree_copy.start()
    for c in range(chunks):
        own_copy(c).wait()

    @pl.loop(0, half)
    def _(i):
        block = REACH * block_rows + rep * half + i
        own = jnp.concatenate([win[c][block] for c in range(chunks)], axis=1)
        base[i] = jnp.dot(own, w_self[...], preferred_element_type=jnp.float32) + bias[...]

    degree_copy.wait()
    inverses = 1.0 / jnp.maximum(own_degrees + degree_in[...], 1.0)

    @pl.loop(0, half)
    def _(i):
        one = jnp.sum(jnp.where(lane == i, inverses, 0.0), axis=1, keepdims=True)
        inverse[i] = jnp.broadcast_to(one, (edge, LANES))

    def aggregate(c, b):
        used = live[0, b] - first_slot
        total = jnp.zeros((edge, LANES), jnp.float32)
        shift = (me - REACH) * block_rows

        def source(s):
            return win[c][zero_block + within(s, used) * (columns[b, s] - shift - zero_block)]

        for s in range(0, slots, 2):
            left = jnp.concatenate([tiles[b, s], tiles[b, s + 1]], axis=1)
            right = jnp.concatenate([source(s), source(s + 1)], axis=0)
            total += jnp.dot(left, right, preferred_element_type=jnp.float32)
        return total

    def finish(c, i):
        part_copy(c, i).wait_recv()
        total = own_totals[c, i] + partial_in[c, i].astype(jnp.float32)
        mean = (total * inverse[i]).astype(jnp.bfloat16)
        return base[i] + jnp.dot(
            mean, w_neigh[pl.ds(c * LANES, LANES), :], preferred_element_type=jnp.float32
        )

    for c in range(chunks):

        @pl.when(relay_out)
        def _():
            for k in range(PIECES):
                arrived(1 - core, c, k)
                relay(c, k).start()

        @pl.when(relay_in)
        def _():
            for k in range(PIECES):
                arrived(core, c, k)
                arrived(3, c, k)

        for k in range(PIECES):
            arrived(2, c, k)

        @pl.loop(0, half)
        def _(i):
            partial_out[c, i] = aggregate(c, other * half + i).astype(jnp.bfloat16)

            @pl.when(i > 0)
            def _():
                part_copy(c, i - 1).start()

        @pl.loop(0, half)
        def _(i):
            own_totals[c, i] = aggregate(c, rep * half + i)

            @pl.when(i == 0)
            def _():
                part_copy(c, half - 1).start()

        @pl.loop(0, half)
        def _(i):
            if c < chunks - 1:
                base[i] = finish(c, i)
            else:
                rows = pl.ds(pl.multiple_of(i * edge, edge), edge)
                out[rows, :] = jnp.maximum(finish(c, i), 0.0).astype(out.dtype)

    for c in range(chunks):
        for k in range(PIECES):

            @pl.when(has_next)
            def _():
                to_next(c, k).wait_send()

            @pl.when(has_prev)
            def _():
                to_prev(c, k).wait_send()

            to_mate(c, k).wait_send()

            @pl.when(relay_out)
            def _():
                relay(c, k).wait_send()

        @pl.loop(0, half)
        def _(i):
            part_copy(c, i).wait_send()


def local(row_total, features, adjacency, columns, live, w_self, w_neigh, bias):
    block_rows, slots, edge, _ = adjacency.shape
    node_rows, width = features.shape
    chunks, half = width // LANES, block_rows // 2
    dma = pltpu.SemaphoreType.DMA
    hbm = pl.BlockSpec(memory_space=pl.ANY)
    vmem = pl.BlockSpec(memory_space=pltpu.VMEM)
    smem = pl.BlockSpec(memory_space=pltpu.SMEM)
    window = pltpu.VMEM(((2 * REACH + 1) * block_rows + 1, edge, LANES), jnp.bfloat16)
    return pl.pallas_call(
        functools.partial(kernel, row_total),
        out_shape=jax.ShapeDtypeStruct((node_rows // 2, width), jnp.bfloat16),
        in_specs=[hbm, hbm, smem, smem, vmem, vmem, vmem],
        out_specs=vmem,
        scratch_shapes=[
            window,
            window,
            pltpu.VMEM(adjacency.shape, jnp.bfloat16),
            pltpu.VMEM((chunks, half, edge, LANES), jnp.bfloat16),
            pltpu.VMEM((chunks, half, edge, LANES), jnp.bfloat16),
            pltpu.VMEM((chunks, half, edge, LANES), jnp.float32),
            pltpu.VMEM((half, edge, width), jnp.float32),
            pltpu.VMEM((half, edge, LANES), jnp.float32),
            pltpu.VMEM((edge, LANES), jnp.float32),
            pltpu.VMEM((edge, LANES), jnp.float32),
            dma((block_rows,)),
            dma((chunks,)),
            dma((4, chunks, PIECES)),
            dma((4, chunks, PIECES)),
            dma((chunks, half)),
            dma((chunks, half)),
            dma((2,)),
        ],
        compiler_params=pltpu.CompilerParams(
            collective_id=0, has_side_effects=True, vmem_limit_bytes=60 << 20
        ),
    )(
        features.reshape(block_rows, edge, width), adjacency, columns, live.reshape(1, block_rows),
        w_self, w_neigh, bias.reshape(1, width),
    )


def solution(mesh):
    placed = (P("row", None), P("row", "rep", None, None), P("row", "rep"), P("row"), P(), P(), P())
    return jax.shard_map(
        functools.partial(local, mesh.shape["row"]),
        mesh=mesh, in_specs=placed, out_specs=P(("row", "rep"), None), check_vma=False,
    )
```

time: 238 us -> 44.7 us (0.19); the launches traced: 233 us -> 44.5 us
  local copies, waits for them, and re-layouts: 66 us -> 1.87 us
  waiting for transfers between devices: 62.7 us -> 0 us
  Pallas kernels: 0 us -> 42.7 us
  matrix products: 38.1 us -> 0 us
  other arithmetic: 35 us -> 0 us
  between operations: 14.2 us -> 0.01 us
  starting transfers between devices: 11.5 us -> 0 us
  blocking collectives: 5.01 us -> 0 us
    gather x16 -> x0, local copies, waits for them, and re-layouts: 50.2 us -> none  [one_row(): source = window[row_index]]
    pallas_call x0 -> x1, Pallas kernels: none -> 42.7 us  [local(): pl.pallas_call(functools.partial(kernel, row_total), out_shape=jax.ShapeD...]
    dot_general x18 -> x0, matrix products: 38.1 us -> none  [the longest x16 35.4 us: one_row(): jnp.einsum('sij,sjf->if', masked, source, preferred_element_type=jnp.floa...]
    ppermute x4 -> x0, waiting for transfers between devices: 36.3 us -> none  [shifted(): return lax.ppermute(block, axis, route)]
    reduce_scatter x1 -> x0, waiting for transfers between devices: 26.4 us -> none  [local(): lax.psum_scatter(totals, 'rep', scatter_dimension=0, tiled=True)]
    reduce_sum x16 -> x0, other arithmetic: 23.3 us -> none  [one_row(): degree = jnp.sum(masked, axis=(0, 2), dtype=jnp.float32)]
    ppermute x4 -> x0, starting transfers between devices: 11.5 us -> none  [shifted(): return lax.ppermute(block, axis, route)]
    lt x16 -> x0, other arithmetic: 10 us -> none  [one_row(): live_slots = jnp.arange(slot_total, dtype=jnp.int32) < row_count]
  transfers between devices with their start and end apart: 5 -> 0, of which waited for: 4 -> 0; matrix products, arithmetic and copies ran while one was open for 2% -> 0% of each run, Pallas kernels for 0% -> 0%
where the time goes in v1:
time: 44.7 us; the launch traced here: 44.5 us
  Pallas kernels  42.7 us (96%)
  local copies, waits for them, and re-layouts  1.87 us (4%)
    pallas_call x1, Pallas kernels, local(): pl.pallas_call(functools.partial(kernel, row_total), out_shape=jax.ShapeD...  42.7 us
    unnamed x1, local copies, waits for them, and re-layouts  1.87 us

profile of v1, /device:TPU:102, one launch (start us, length us, event | category | flops | bytes accessed | tf_op | source)
XLA Modules:
  0.0 44.5 jit_solution(14628503476771445365)
XLA Ops:
  0.0 42.7 %shard_map.73 = bf16[1024,256]{1,0:T(8,128)(2,1)} custom-call(bf16[16,128,256]{2,1,0:T(8,128)(2,1)} %bitcast.3, bf16[16,24,128,128]{3,2,1,0:T(8,128)(2,1)} %adjacency.1, s32[16,24]{1,0:T(8,128)} %columns.1, s32[1,16]{1,0:T(1,128)} %bitcast.5, bf16[256,256]{1,0:T(8,128)(2,1)} %w_self.1, bf16[256,256]{1,0:T(8,128)(2,1)} %w_neigh.1, f32[1,256]{1,0:T(1,128)} %bitcast.4), custom_call_target="tpu_custom_call" | custom-call | tf_op jit(solution)/shard_map/pallas_call | solution.py:268
  42.7 1.9 %copy.9 = bf16[1024,256]{1,0:T(8,128)(2,1)} copy(bf16[1024,256]{1,0:T(8,128)(2,1)} %shard_map.73) | data formatting | bytes 1048576

commit v2 on v1

--- a/solution.py
+++ b/solution.py
@@ -9,7 +9,8 @@
 
 REACH = 2
 LANES = 128
-PIECES = 4
+SHARED = (5, 3)
+REST = ((3, 3), (5, 3, 2))
 MESH = pl.DeviceIdType.MESH
 
 
@@ -21,7 +22,6 @@
     block_rows, slots, edge, _ = tiles.shape
     width = feats.shape[2]
     chunks = width // LANES
-    piece = block_rows // PIECES
     half = block_rows // 2
     zero_block = (2 * REACH + 1) * block_rows
     win = (win_low, win_high)
@@ -50,34 +50,86 @@
             own_sem.at[c],
         )
 
-    def remote(flow, c, k, src, slot, device):
+    def span(c, j, side):
+        shared, rest = SHARED[c], REST[c]
+        if j == 0:
+            return (1 - side) * shared, shared
+        if j <= len(rest):
+            return 2 * shared + sum(rest[: j - 1]), rest[j - 1]
+        return side * shared, shared
+
+    def remote(flow, c, j, src, slot, start, size, device):
         return pltpu.make_async_remote_copy(
             src_ref=src,
-            dst_ref=win[c].at[pl.ds(slot * block_rows + k * piece, piece)],
-            send_sem=send_sem.at[flow, c, k],
-            recv_sem=recv_sem.at[flow, c, k],
+            dst_ref=win[c].at[pl.ds(slot * block_rows + start, size)],
+            send_sem=send_sem.at[flow, c, j],
+            recv_sem=recv_sem.at[flow, c, j],
             device_id=device,
             device_id_type=MESH,
         )
 
-    def own_piece(c, k):
-        return feats.at[pl.ds(k * piece, piece), :, pl.ds(c * LANES, LANES)]
-
-    def to_next(c, k):
-        return remote(0, c, k, own_piece(c, k), 0, (me + 2, rep_next))
-
-    def to_prev(c, k):
-        return remote(1, c, k, own_piece(c, k), 4, (me - 2, rep_prev))
-
-    def to_mate(c, k):
-        return remote(2, c, k, own_piece(c, k), 1 + 2 * core, (mate, rep))
-
-    def relay(c, k):
-        start = (4 - 4 * core) * block_rows + k * piece
-        return remote(3, c, k, win[c].at[pl.ds(start, piece)], 3 - 2 * core, (mate, rep))
-
-    def arrived(flow, c, k):
-        remote(flow, c, k, own_piece(c, k), 0, (mate, rep)).wait_recv()
+    def own_piece(c, start, size):
+        return feats.at[pl.ds(start, size), :, pl.ds(c * LANES, LANES)]
+
+    def held(c, slot, start, size):
+        return win[c].at[pl.ds(slot * block_rows + start, size)]
+
+    def to_next(c, j):
+        start, size = span(c, j, rep_next)
+        return remote(0, c, j, own_piece(c, start, size), 0, start, size, (me + 2, rep_next))
+
+    def to_prev(c, j):
+        start, size = span(c, j, rep_prev)
+        return remote(1, c, j, own_piece(c, start, size), 4, start, size, (me - 2, rep_prev))
+
+    def to_mate(c):
+        whole = own_piece(c, 0, block_rows)
+        return remote(2, c, 0, whole, 1 + 2 * core, 0, block_rows, (mate, rep))
+
+    def across(flow, c):
+        start, size = span(c, 0, rep)
+        j, slot = len(REST[c]) + 1, 4 * flow
+        return remote(flow, c, j, held(c, slot, start, size), slot, start, size, (me, other))
+
+    def relay(c, j):
+        start, size = span(c, j, rep)
+        src = held(c, 4 - 4 * core, start, size)
+        return remote(3, c, j, src, 3 - 2 * core, start, size, (mate, rep))
+
+    def arrived(flow, c, j):
+        start, size = span(c, j, rep)
+        remote(flow, c, j, held(c, 0, start, size), 0, start, size, (mate, rep)).wait_recv()
+
+    def forward(c):
+        @pl.when(relay_out)
+        def _():
+            arrived(1 - core, c, 0)
+            across(1 - core, c).start()
+            relay(c, 0).start()
+
+        @pl.when(relay_in)
+        def _():
+            arrived(core, c, 0)
+            across(core, c).start()
+
+    def complete(c):
+        last = len(REST[c])
+        order = [*range(1, last), last + 1, last]
+
+        @pl.when(relay_out)
+        def _():
+            for j in order:
+                arrived(1 - core, c, j)
+                relay(c, j).start()
+
+        @pl.when(relay_in)
+        def _():
+            for j in order:
+                arrived(core, c, j)
+            for j in [0, *order]:
+                arrived(3, c, j)
+
+        to_mate(c).wait_recv()
 
     def part_copy(c, i):
         return pltpu.make_async_remote_copy(
@@ -98,37 +150,37 @@
         device_id_type=MESH,
     )
 
+    barrier = pltpu.get_barrier_semaphore()
+    pl.semaphore_signal(barrier, inc=1, device_id=(mate, rep), device_id_type=MESH)
+    pl.semaphore_signal(barrier, inc=1, device_id=(me, other), device_id_type=MESH)
+
+    @pl.when(has_next)
+    def _():
+        pl.semaphore_signal(barrier, inc=1, device_id=(me + 2, rep_next), device_id_type=MESH)
+
+    @pl.when(has_prev)
+    def _():
+        pl.semaphore_signal(barrier, inc=1, device_id=(me - 2, rep_prev), device_id_type=MESH)
+
     for c in range(chunks):
         own_copy(c).start()
     for b in range(block_rows):
         tile_copy(b).start()
 
-    barrier = pltpu.get_barrier_semaphore()
-    pl.semaphore_signal(barrier, inc=1, device_id=(mate, rep), device_id_type=MESH)
-    pl.semaphore_signal(barrier, inc=1, device_id=(me, other), device_id_type=MESH)
-
-    @pl.when(has_next)
-    def _():
-        pl.semaphore_signal(barrier, inc=1, device_id=(me + 2, rep_next), device_id_type=MESH)
-
-    @pl.when(has_prev)
-    def _():
-        pl.semaphore_signal(barrier, inc=1, device_id=(me - 2, rep_prev), device_id_type=MESH)
-
     pl.semaphore_wait(barrier, 2 + has_next.astype(jnp.int32) + has_prev.astype(jnp.int32))
 
     for c in range(chunks):
-        for k in range(PIECES):
+        for j in range(len(REST[c]) + 1):
 
             @pl.when(has_next)
             def _():
-                to_next(c, k).start()
+                to_next(c, j).start()
 
             @pl.when(has_prev)
             def _():
-                to_prev(c, k).start()
-
-            to_mate(c, k).start()
+                to_prev(c, j).start()
+
+        to_mate(c).start()
 
     lane = lax.broadcasted_iota(jnp.int32, (edge, LANES), 1)
     first_slot = rep * slots
@@ -138,20 +190,24 @@
     def within(s, used):
         return jnp.minimum(jnp.maximum(used - s, 0), 1)
 
-    def degree_of(b, i, held):
+    def degree_of(b, i, found):
         tile_copy(b).wait()
         used = live[0, b] - first_slot
         total = jnp.zeros((edge, edge), jnp.float32)
         for s in range(slots):
             total += tiles[b, s].astype(jnp.float32) * within(s, used).astype(jnp.float32)
-        return jnp.where(lane == i, jnp.sum(total, axis=1, keepdims=True), held)
+        return jnp.where(lane == i, jnp.sum(total, axis=1, keepdims=True), found)
 
     no_degrees = jnp.zeros((edge, LANES), jnp.float32)
-    degree_out[...] = lax.fori_loop(
-        0, half, lambda i, held: degree_of(other * half + i, i, held), no_degrees
-    )
+    def packed(row):
+        return jnp.transpose(row)[:half, :]
+
+    degree_out[...] = packed(
+        lax.fori_loop(0, half, lambda i, d: degree_of(other * half + i, i, d), no_degrees)
+    )
+    forward(0)
     own_degrees = lax.fori_loop(
-        0, half, lambda i, held: degree_of(rep * half + i, i, held), no_degrees
+        0, half, lambda i, d: degree_of(rep * half + i, i, d), no_degrees
     )
     degree_copy.start()
     for c in range(chunks):
@@ -162,14 +218,6 @@
         block = REACH * block_rows + rep * half + i
         own = jnp.concatenate([win[c][block] for c in range(chunks)], axis=1)
         base[i] = jnp.dot(own, w_self[...], preferred_element_type=jnp.float32) + bias[...]
-
-    degree_copy.wait()
-    inverses = 1.0 / jnp.maximum(own_degrees + degree_in[...], 1.0)
-
-    @pl.loop(0, half)
-    def _(i):
-        one = jnp.sum(jnp.where(lane == i, inverses, 0.0), axis=1, keepdims=True)
-        inverse[i] = jnp.broadcast_to(one, (edge, LANES))
 
     def aggregate(c, b):
         used = live[0, b] - first_slot
@@ -193,23 +241,7 @@
             mean, w_neigh[pl.ds(c * LANES, LANES), :], preferred_element_type=jnp.float32
         )
 
-    for c in range(chunks):
-
-        @pl.when(relay_out)
-        def _():
-            for k in range(PIECES):
-                arrived(1 - core, c, k)
-                relay(c, k).start()
-
-        @pl.when(relay_in)
-        def _():
-            for k in range(PIECES):
-                arrived(core, c, k)
-                arrived(3, c, k)
-
-        for k in range(PIECES):
-            arrived(2, c, k)
-
+    def send_partials(c):
         @pl.loop(0, half)
         def _(i):
             partial_out[c, i] = aggregate(c, other * half + i).astype(jnp.bfloat16)
@@ -218,38 +250,67 @@
             def _():
                 part_copy(c, i - 1).start()
 
+    def keep_own(c):
+        part_copy(c, half - 1).start()
+
         @pl.loop(0, half)
         def _(i):
             own_totals[c, i] = aggregate(c, rep * half + i)
 
-            @pl.when(i == 0)
-            def _():
-                part_copy(c, half - 1).start()
-
-        @pl.loop(0, half)
-        def _(i):
-            if c < chunks - 1:
-                base[i] = finish(c, i)
-            else:
-                rows = pl.ds(pl.multiple_of(i * edge, edge), edge)
-                out[rows, :] = jnp.maximum(finish(c, i), 0.0).astype(out.dtype)
-
-    for c in range(chunks):
-        for k in range(PIECES):
+    complete(0)
+    send_partials(0)
+    forward(1)
+    keep_own(0)
+
+    degree_copy.wait()
+    others = jnp.concatenate(
+        [degree_in[...], jnp.zeros((edge - half, LANES), jnp.float32)], axis=0
+    )
+    inverses = 1.0 / jnp.maximum(own_degrees + jnp.transpose(others), 1.0)
+
+    @pl.loop(0, half)
+    def _(i):
+        one = jnp.sum(jnp.where(lane == i, inverses, 0.0), axis=1, keepdims=True)
+        inverse[i] = jnp.broadcast_to(one, (edge, LANES))
+
+    complete(1)
+    send_partials(1)
+    keep_own(1)
+
+    @pl.loop(0, half)
+    def _(i):
+        base[i] = finish(0, i)
+
+    @pl.loop(0, half)
+    def _(i):
+        rows = pl.ds(pl.multiple_of(i * edge, edge), edge)
+        out[rows, :] = jnp.maximum(finish(1, i), 0.0).astype(out.dtype)
+
+    for c in range(chunks):
+        for j in range(len(REST[c]) + 1):
 
             @pl.when(has_next)
             def _():
-                to_next(c, k).wait_send()
+                to_next(c, j).wait_send()
 
             @pl.when(has_prev)
             def _():
-                to_prev(c, k).wait_send()
-
-            to_mate(c, k).wait_send()
-
-            @pl.when(relay_out)
-            def _():
-                relay(c, k).wait_send()
+                to_prev(c, j).wait_send()
+
+        to_mate(c).wait_send()
+
+        @pl.when(has_prev)
+        def _():
+            across(0, c).wait_send()
+
+        @pl.when(has_next)
+        def _():
+            across(1, c).wait_send()
+
+        @pl.when(relay_out)
+        def _():
+            for j in range(len(REST[c]) + 2):
+                relay(c, j).wait_send()
 
         @pl.loop(0, half)
         def _(i):
@@ -260,6 +321,7 @@
     block_rows, slots, edge, _ = adjacency.shape
     node_rows, width = features.shape
     chunks, half = width // LANES, block_rows // 2
+    pieces = 2 + max(len(rest) for rest in REST)
     dma = pltpu.SemaphoreType.DMA
     hbm = pl.BlockSpec(memory_space=pl.ANY)
     vmem = pl.BlockSpec(memory_space=pltpu.VMEM)
@@ -279,12 +341,12 @@
             pltpu.VMEM((chunks, half, edge, LANES), jnp.float32),
             pltpu.VMEM((half, edge, width), jnp.float32),
             pltpu.VMEM((half, edge, LANES), jnp.float32),
-            pltpu.VMEM((edge, LANES), jnp.float32),
-            pltpu.VMEM((edge, LANES), jnp.float32),
+            pltpu.VMEM((half, LANES), jnp.float32),
+            pltpu.VMEM((half, LANES), jnp.float32),
             dma((block_rows,)),
             dma((chunks,)),
-            dma((4, chunks, PIECES)),
-            dma((4, chunks, PIECES)),
+            dma((4, chunks, pieces)),
+            dma((4, chunks, pieces)),
             dma((chunks, half)),
             dma((chunks, half)),
             dma((2,)),

time: 44.7 us -> 44.3 us (level)
  Pallas kernels: 42.7 us -> 42.2 us
where the time goes in v2:
time: 44.3 us; the launch traced here: 44.1 us
  Pallas kernels  42.2 us (95%)
  local copies, waits for them, and re-layouts  1.87 us (4%)
    pallas_call x1, Pallas kernels, local(): pl.pallas_call(functools.partial(kernel, row_total), out_shape=jax.ShapeD...  42.2 us
    unnamed x1, local copies, waits for them, and re-layouts  1.87 us

profile of v2, /device:TPU:102, one launch (start us, length us, event | category | flops | bytes accessed | tf_op | source)
XLA Modules:
  0.0 44.1 jit_solution(4184573860832528362)
XLA Ops:
  0.0 42.2 %shard_map.73 = bf16[1024,256]{1,0:T(8,128)(2,1)} custom-call(bf16[16,128,256]{2,1,0:T(8,128)(2,1)} %bitcast.3, bf16[16,24,128,128]{3,2,1,0:T(8,128)(2,1)} %adjacency.1, s32[16,24]{1,0:T(8,128)} %columns.1, s32[1,16]{1,0:T(1,128)} %bitcast.5, bf16[256,256]{1,0:T(8,128)(2,1)} %w_self.1, bf16[256,256]{1,0:T(8,128)(2,1)} %w_neigh.1, f32[1,256]{1,0:T(1,128)} %bitcast.4), custom_call_target="tpu_custom_call" | custom-call | tf_op jit(solution)/shard_map/pallas_call | solution.py:330
  42.2 1.9 %copy.9 = bf16[1024,256]{1,0:T(8,128)(2,1)} copy(bf16[1024,256]{1,0:T(8,128)(2,1)} %shard_map.73) | data formatting | bytes 1048576

commit v3 on v2

--- a/solution.py
+++ b/solution.py
@@ -9,8 +9,8 @@
 
 REACH = 2
 LANES = 128
-SHARED = (5, 3)
-REST = ((3, 3), (5, 3, 2))
+SHARED = ((2, 2), (2,))
+REST = ((4, 3, 1), (4, 4, 3, 1))
 MESH = pl.DeviceIdType.MESH
 
 
@@ -52,11 +52,14 @@
 
     def span(c, j, side):
         shared, rest = SHARED[c], REST[c]
-        if j == 0:
-            return (1 - side) * shared, shared
-        if j <= len(rest):
-            return 2 * shared + sum(rest[: j - 1]), rest[j - 1]
-        return side * shared, shared
+        count, total = len(shared), sum(shared)
+        if j < count:
+            return (1 - side) * total + sum(shared[:j]), shared[j]
+        j -= count
+        if j < len(rest):
+            return 2 * total + sum(rest[:j]), rest[j]
+        j -= len(rest)
+        return side * total + sum(shared[:j]), shared[j]
 
     def remote(flow, c, j, src, slot, start, size, device):
         return pltpu.make_async_remote_copy(
@@ -86,10 +89,11 @@
         whole = own_piece(c, 0, block_rows)
         return remote(2, c, 0, whole, 1 + 2 * core, 0, block_rows, (mate, rep))
 
-    def across(flow, c):
-        start, size = span(c, 0, rep)
-        j, slot = len(REST[c]) + 1, 4 * flow
-        return remote(flow, c, j, held(c, slot, start, size), slot, start, size, (me, other))
+    def across(flow, c, j):
+        start, size = span(c, j, rep)
+        slot = 4 * flow
+        there = len(SHARED[c]) + len(REST[c]) + j
+        return remote(flow, c, there, held(c, slot, start, size), slot, start, size, (me, other))
 
     def relay(c, j):
         start, size = span(c, j, rep)
@@ -100,33 +104,40 @@
         start, size = span(c, j, rep)
         remote(flow, c, j, held(c, 0, start, size), 0, start, size, (mate, rep)).wait_recv()
 
+    def direct(c):
+        return range(len(SHARED[c]) + len(REST[c]))
+
     def forward(c):
+        for j in range(len(SHARED[c])):
+
+            @pl.when(relay_out)
+            def _():
+                arrived(1 - core, c, j)
+                across(1 - core, c, j).start()
+                relay(c, j).start()
+
+            @pl.when(relay_in)
+            def _():
+                arrived(core, c, j)
+                across(core, c, j).start()
+
+    def pass_on(c, pieces):
         @pl.when(relay_out)
         def _():
-            arrived(1 - core, c, 0)
-            across(1 - core, c).start()
-            relay(c, 0).start()
-
-        @pl.when(relay_in)
-        def _():
-            arrived(core, c, 0)
-            across(core, c).start()
-
-    def complete(c):
-        last = len(REST[c])
-        order = [*range(1, last), last + 1, last]
-
-        @pl.when(relay_out)
-        def _():
-            for j in order:
+            for j in pieces:
                 arrived(1 - core, c, j)
                 relay(c, j).start()
 
+    def complete(c, passed):
+        count, sent = len(SHARED[c]), len(direct(c))
+        inbound = range(sent, sent + count)
+        pass_on(c, [*range(count + passed, sent - 1), *inbound, sent - 1])
+
         @pl.when(relay_in)
         def _():
-            for j in order:
+            for j in range(count, sent + count):
                 arrived(core, c, j)
-            for j in [0, *order]:
+            for j in range(sent + count):
                 arrived(3, c, j)
 
         to_mate(c).wait_recv()
@@ -170,7 +181,7 @@
     pl.semaphore_wait(barrier, 2 + has_next.astype(jnp.int32) + has_prev.astype(jnp.int32))
 
     for c in range(chunks):
-        for j in range(len(REST[c]) + 1):
+        for j in direct(c):
 
             @pl.when(has_next)
             def _():
@@ -202,10 +213,11 @@
     def packed(row):
         return jnp.transpose(row)[:half, :]
 
+    forward(0)
     degree_out[...] = packed(
         lax.fori_loop(0, half, lambda i, d: degree_of(other * half + i, i, d), no_degrees)
     )
-    forward(0)
+    pass_on(0, [len(SHARED[0])])
     own_degrees = lax.fori_loop(
         0, half, lambda i, d: degree_of(rep * half + i, i, d), no_degrees
     )
@@ -257,9 +269,9 @@
         def _(i):
             own_totals[c, i] = aggregate(c, rep * half + i)
 
-    complete(0)
+    complete(0, 1)
+    forward(1)
     send_partials(0)
-    forward(1)
     keep_own(0)
 
     degree_copy.wait()
@@ -273,7 +285,7 @@
         one = jnp.sum(jnp.where(lane == i, inverses, 0.0), axis=1, keepdims=True)
         inverse[i] = jnp.broadcast_to(one, (edge, LANES))
 
-    complete(1)
+    complete(1, 0)
     send_partials(1)
     keep_own(1)
 
@@ -287,7 +299,7 @@
         out[rows, :] = jnp.maximum(finish(1, i), 0.0).astype(out.dtype)
 
     for c in range(chunks):
-        for j in range(len(REST[c]) + 1):
+        for j in direct(c):
 
             @pl.when(has_next)
             def _():
@@ -301,15 +313,17 @@
 
         @pl.when(has_prev)
         def _():
-            across(0, c).wait_send()
+            for j in range(len(SHARED[c])):
+                across(0, c, j).wait_send()
 
         @pl.when(has_next)
         def _():
-            across(1, c).wait_send()
+            for j in range(len(SHARED[c])):
+                across(1, c, j).wait_send()
 
         @pl.when(relay_out)
         def _():
-            for j in range(len(REST[c]) + 2):
+            for j in range(len(SHARED[c]) + len(direct(c))):
                 relay(c, j).wait_send()
 
         @pl.loop(0, half)
@@ -321,7 +335,7 @@
     block_rows, slots, edge, _ = adjacency.shape
     node_rows, width = features.shape
     chunks, half = width // LANES, block_rows // 2
-    pieces = 2 + max(len(rest) for rest in REST)
+    pieces = max(2 * len(a) + len(b) for a, b in zip(SHARED, REST))
     dma = pltpu.SemaphoreType.DMA
     hbm = pl.BlockSpec(memory_space=pl.ANY)
     vmem = pl.BlockSpec(memory_space=pltpu.VMEM)

time: 44.3 us -> 41.9 us (0.946)
  Pallas kernels: 42.2 us -> 39.7 us
    pallas_call x1, Pallas kernels: 42.2 us -> 39.7 us  [local(): pl.pallas_call(functools.partial(kernel, row_total), out_shape=jax.ShapeD...]
where the time goes in v3:
time: 41.9 us; the launch traced here: 41.6 us
  Pallas kernels  39.7 us (95%)
  local copies, waits for them, and re-layouts  1.87 us (4%)
    pallas_call x1, Pallas kernels, local(): pl.pallas_call(functools.partial(kernel, row_total), out_shape=jax.ShapeD...  39.7 us
    unnamed x1, local copies, waits for them, and re-layouts  1.87 us

profile of v3, /device:TPU:102, one launch (start us, length us, event | category | flops | bytes accessed | tf_op | source)
XLA Modules:
  0.0 41.6 jit_solution(1426888222849478180)
XLA Ops:
  0.0 39.7 %shard_map.73 = bf16[1024,256]{1,0:T(8,128)(2,1)} custom-call(bf16[16,128,256]{2,1,0:T(8,128)(2,1)} %bitcast.3, bf16[16,24,128,128]{3,2,1,0:T(8,128)(2,1)} %adjacency.1, s32[16,24]{1,0:T(8,128)} %columns.1, s32[1,16]{1,0:T(1,128)} %bitcast.5, bf16[256,256]{1,0:T(8,128)(2,1)} %w_self.1, bf16[256,256]{1,0:T(8,128)(2,1)} %w_neigh.1, f32[1,256]{1,0:T(1,128)} %bitcast.4), custom_call_target="tpu_custom_call" | custom-call | tf_op jit(solution)/shard_map/pallas_call | solution.py:344
  39.7 1.9 %copy.9 = bf16[1024,256]{1,0:T(8,128)(2,1)} copy(bf16[1024,256]{1,0:T(8,128)(2,1)} %shard_map.73) | data formatting | bytes 1048576

commit v4 on v3

--- a/solution.py
+++ b/solution.py
@@ -15,9 +15,10 @@
 
 
 def kernel(
-    row_total, feats, adjacency, columns, live, w_self, w_neigh, bias, out,
+    row_total, feats, adjacency, columns_hbm, live_hbm, w_self_hbm, w_neigh_hbm, bias_hbm, out_hbm,
     win_low, win_high, tiles, partial_out, partial_in, own_totals, base, inverse, degree_out, degree_in,
     tile_sem, own_sem, send_sem, recv_sem, part_send, part_recv, degree_sems,
+    columns, live, w_self, w_neigh, bias, small_sem, out, out_sem,
 ):
     block_rows, slots, edge, _ = tiles.shape
     width = feats.shape[2]
@@ -161,6 +162,13 @@
         device_id_type=MESH,
     )
 
+    small = [
+        pltpu.make_async_copy(source, target, small_sem.at[n])
+        for n, (source, target) in enumerate((
+            (live_hbm, live), (columns_hbm, columns), (w_self_hbm, w_self), (w_neigh_hbm, w_neigh),
+            (bias_hbm, bias),
+        ))
+    ]
     barrier = pltpu.get_barrier_semaphore()
     pl.semaphore_signal(barrier, inc=1, device_id=(mate, rep), device_id_type=MESH)
     pl.semaphore_signal(barrier, inc=1, device_id=(me, other), device_id_type=MESH)
@@ -175,6 +183,8 @@
 
     for c in range(chunks):
         own_copy(c).start()
+    for copy in small:
+        copy.start()
     for b in range(block_rows):
         tile_copy(b).start()
 
@@ -214,6 +224,8 @@
         return jnp.transpose(row)[:half, :]
 
     forward(0)
+    for copy in small:
+        copy.wait()
     degree_out[...] = packed(
         lax.fori_loop(0, half, lambda i, d: degree_of(other * half + i, i, d), no_degrees)
     )
@@ -293,10 +305,15 @@
     def _(i):
         base[i] = finish(0, i)
 
+    def out_copy(i):
+        rows = pl.ds(pl.multiple_of(i * edge, edge), edge)
+        return pltpu.make_async_copy(out.at[rows], out_hbm.at[rows], out_sem.at[i])
+
     @pl.loop(0, half)
     def _(i):
         rows = pl.ds(pl.multiple_of(i * edge, edge), edge)
         out[rows, :] = jnp.maximum(finish(1, i), 0.0).astype(out.dtype)
+        out_copy(i).start()
 
     for c in range(chunks):
         for j in direct(c):
@@ -329,6 +346,10 @@
         @pl.loop(0, half)
         def _(i):
             part_copy(c, i).wait_send()
+
+    @pl.loop(0, half)
+    def _(i):
+        out_copy(i).wait()
 
 
 def local(row_total, features, adjacency, columns, live, w_self, w_neigh, bias):
@@ -338,14 +359,12 @@
     pieces = max(2 * len(a) + len(b) for a, b in zip(SHARED, REST))
     dma = pltpu.SemaphoreType.DMA
     hbm = pl.BlockSpec(memory_space=pl.ANY)
-    vmem = pl.BlockSpec(memory_space=pltpu.VMEM)
-    smem = pl.BlockSpec(memory_space=pltpu.SMEM)
     window = pltpu.VMEM(((2 * REACH + 1) * block_rows + 1, edge, LANES), jnp.bfloat16)
     return pl.pallas_call(
         functools.partial(kernel, row_total),
         out_shape=jax.ShapeDtypeStruct((node_rows // 2, width), jnp.bfloat16),
-        in_specs=[hbm, hbm, smem, smem, vmem, vmem, vmem],
-        out_specs=vmem,
+        in_specs=[hbm] * 7,
+        out_specs=hbm,
         scratch_shapes=[
             window,
             window,
@@ -364,6 +383,14 @@
             dma((chunks, half)),
             dma((chunks, half)),
             dma((2,)),
+            pltpu.SMEM(columns.shape, jnp.int32),
+            pltpu.SMEM((1, block_rows), jnp.int32),
+            pltpu.VMEM(w_self.shape, w_self.dtype),
+            pltpu.VMEM(w_neigh.shape, w_neigh.dtype),
+            pltpu.VMEM((1, width), bias.dtype),
+            dma((5,)),
+            pltpu.VMEM((block_rows * edge // 2, width), jnp.bfloat16),
+            dma((half,)),
         ],
         compiler_params=pltpu.CompilerParams(
             collective_id=0, has_side_effects=True, vmem_limit_bytes=60 << 20

time: 41.9 us -> 40.7 us (0.971)
  Pallas kernels: 39.7 us -> 38.5 us
    pallas_call x1, Pallas kernels: 39.7 us -> 38.5 us  [local(): pl.pallas_call(functools.partial(kernel, row_total), out_shape=jax.ShapeD...]
where the time goes in v4:
time: 40.7 us; the launch traced here: 40.4 us
  Pallas kernels  38.5 us (95%)
  local copies, waits for them, and re-layouts  1.87 us (5%)
    pallas_call x1, Pallas kernels, local(): pl.pallas_call(functools.partial(kernel, row_total), out_shape=jax.ShapeD...  38.5 us
    unnamed x1, local copies, waits for them, and re-layouts  1.87 us

profile of v4, /device:TPU:102, one launch (start us, length us, event | category | flops | bytes accessed | tf_op | source)
XLA Modules:
  0.0 40.4 jit_solution(14108646314978321943)
XLA Ops:
  0.0 38.5 %shard_map.73 = bf16[1024,256]{1,0:T(8,128)(2,1)} custom-call(bf16[16,128,256]{2,1,0:T(8,128)(2,1)} %bitcast.3, bf16[16,24,128,128]{3,2,1,0:T(8,128)(2,1)} %adjacency.1, s32[16,24]{1,0:T(8,128)} %columns_hbm.1, s32[1,16]{1,0:T(1,128)} %bitcast.5, bf16[256,256]{1,0:T(8,128)(2,1)} %w_self_hbm.1, bf16[256,256]{1,0:T(8,128)(2,1)} %w_neigh_hbm.1, f32[1,256]{1,0:T(1,128)} %bitcast.4), custom_call_target="tpu_custom_call" | custom-call | tf_op jit(solution)/shard_map/pallas_call | solution.py:363
  38.5 1.9 %copy.9 = bf16[1024,256]{1,0:T(8,128)(2,1)} copy(bf16[1024,256]{1,0:T(8,128)(2,1)} %shard_map.73) | data formatting | bytes 1048576

commit v5 on v4

--- a/solution.py
+++ b/solution.py
@@ -170,8 +170,6 @@
         ))
     ]
     barrier = pltpu.get_barrier_semaphore()
-    pl.semaphore_signal(barrier, inc=1, device_id=(mate, rep), device_id_type=MESH)
-    pl.semaphore_signal(barrier, inc=1, device_id=(me, other), device_id_type=MESH)
 
     @pl.when(has_next)
     def _():
@@ -180,6 +178,24 @@
     @pl.when(has_prev)
     def _():
         pl.semaphore_signal(barrier, inc=1, device_id=(me - 2, rep_prev), device_id_type=MESH)
+
+    pl.semaphore_signal(barrier, inc=1, device_id=(mate, rep), device_id_type=MESH)
+    pl.semaphore_signal(barrier, inc=1, device_id=(me, other), device_id_type=MESH)
+
+    pl.semaphore_wait(barrier, 2 + has_next.astype(jnp.int32) + has_prev.astype(jnp.int32))
+
+    for c in range(chunks):
+        for j in direct(c):
+
+            @pl.when(has_next)
+            def _():
+                to_next(c, j).start()
+
+            @pl.when(has_prev)
+            def _():
+                to_prev(c, j).start()
+
+        to_mate(c).start()
 
     for c in range(chunks):
         own_copy(c).start()
@@ -187,21 +203,6 @@
         copy.start()
     for b in range(block_rows):
         tile_copy(b).start()
-
-    pl.semaphore_wait(barrier, 2 + has_next.astype(jnp.int32) + has_prev.astype(jnp.int32))
-
-    for c in range(chunks):
-        for j in direct(c):
-
-            @pl.when(has_next)
-            def _():
-                to_next(c, j).start()
-
-            @pl.when(has_prev)
-            def _():
-                to_prev(c, j).start()
-
-        to_mate(c).start()
 
     lane = lax.broadcasted_iota(jnp.int32, (edge, LANES), 1)
     first_slot = rep * slots

time: 40.7 us -> 40.7 us (level)
  no operation moved by 1% of the time
where the time goes in v5:
time: 40.7 us; the launch traced here: 40.4 us
  Pallas kernels  38.5 us (95%)
  local copies, waits for them, and re-layouts  1.87 us (5%)
    pallas_call x1, Pallas kernels, local(): pl.pallas_call(functools.partial(kernel, row_total), out_shape=jax.ShapeD...  38.5 us
    unnamed x1, local copies, waits for them, and re-layouts  1.87 us

profile of v5, /device:TPU:102, one launch (start us, length us, event | category | flops | bytes accessed | tf_op | source)
XLA Modules:
  0.0 40.4 jit_solution(7916205554899566391)
XLA Ops:
  0.0 38.5 %shard_map.73 = bf16[1024,256]{1,0:T(8,128)(2,1)} custom-call(bf16[16,128,256]{2,1,0:T(8,128)(2,1)} %bitcast.3, bf16[16,24,128,128]{3,2,1,0:T(8,128)(2,1)} %adjacency.1, s32[16,24]{1,0:T(8,128)} %columns_hbm.1, s32[1,16]{1,0:T(1,128)} %bitcast.5, bf16[256,256]{1,0:T(8,128)(2,1)} %w_self_hbm.1, bf16[256,256]{1,0:T(8,128)(2,1)} %w_neigh_hbm.1, f32[1,256]{1,0:T(1,128)} %bitcast.4), custom_call_target="tpu_custom_call" | custom-call | tf_op jit(solution)/shard_map/pallas_call | solution.py:364
  38.5 1.9 %copy.9 = bf16[1024,256]{1,0:T(8,128)(2,1)} copy(bf16[1024,256]{1,0:T(8,128)(2,1)} %shard_map.73) | data formatting | bytes 1048576

commit v6 on v5

--- a/solution.py
+++ b/solution.py
@@ -9,8 +9,8 @@
 
 REACH = 2
 LANES = 128
-SHARED = ((2, 2), (2,))
-REST = ((4, 3, 1), (4, 4, 3, 1))
+SHARED = ((3,2),(2,))
+REST = ((3,2,1),(7,4,1))
 MESH = pl.DeviceIdType.MESH
 
 

time: 40.7 us -> 40.5 us (level)
  no operation moved by 1% of the time
where the time goes in v6:
time: 40.5 us; the launch traced here: 40.4 us
  Pallas kernels  38.5 us (95%)
  local copies, waits for them, and re-layouts  1.87 us (5%)
    pallas_call x1, Pallas kernels, local(): pl.pallas_call(functools.partial(kernel, row_total), out_shape=jax.ShapeD...  38.5 us
    unnamed x1, local copies, waits for them, and re-layouts  1.87 us

profile of v6, /device:TPU:102, one launch (start us, length us, event | category | flops | bytes accessed | tf_op | source)
XLA Modules:
  0.0 40.4 jit_solution(10607490303404106398)
XLA Ops:
  0.0 38.5 %shard_map.73 = bf16[1024,256]{1,0:T(8,128)(2,1)} custom-call(bf16[16,128,256]{2,1,0:T(8,128)(2,1)} %bitcast.3, bf16[16,24,128,128]{3,2,1,0:T(8,128)(2,1)} %adjacency.1, s32[16,24]{1,0:T(8,128)} %columns_hbm.1, s32[1,16]{1,0:T(1,128)} %bitcast.5, bf16[256,256]{1,0:T(8,128)(2,1)} %w_self_hbm.1, bf16[256,256]{1,0:T(8,128)(2,1)} %w_neigh_hbm.1, f32[1,256]{1,0:T(1,128)} %bitcast.4), custom_call_target="tpu_custom_call" | custom-call | tf_op jit(solution)/shard_map/pallas_call | solution.py:364
  38.5 1.9 %copy.9 = bf16[1024,256]{1,0:T(8,128)(2,1)} copy(bf16[1024,256]{1,0:T(8,128)(2,1)} %shard_map.73) | data formatting | bytes 1048576
